TPU v7x, 128 devices: a whole 4x4x4 slice. The times are simulated.
128 devices in a mesh: sub: 32 (over x, y_hi, z), lib: 4 (over y_lo, core).
Axes of the slice: x: 4, y: 4 (y_hi: 2, y_lo: 2; y = y_hi * 2 + y_lo), z: 4, core: 2. Of those that a mesh axis runs over, the one named last changes fastest.
Arguments:
- snap_start: bfloat16 [4, 256, 128, 256], P(None, 'sub'), may hold values from -20 to 20
- snap_end: bfloat16 [4, 256, 128, 256], P(None, 'sub'), may hold values from -20 to 20
- exponents: int32 [512, 7], P('lib'), may hold values from 0 to 2, as said below
Outputs:
- coefficients: float32 [4, 512], P(None, 'lib')
- fitted: float32 [4, 16384], P(None, ('sub', 'lib'))
Inputs may be any that keep to these rules, and one draw needn't show every extreme that they name: Each row holds four field exponents of 0 to 2 with total degree 1 to 3, then three derivative orders of 0 to 2; rows are distinct, each of the 30 such monomials appears in one row whose derivative orders are all zero, and each of the four fields to the first power alone appears with derivative orders (0, 0, 1) and with (0, 1, 1).
All inputs are finite; a program needn't handle non-finite values.
Results may differ from a plain program's by a relative error of at most 0.0024.
Values may be sent and summed in bfloat16 or wider, within the bound.
A program may use at most 64 MiB of HBM per device.

v0:
```python
import jax
import jax.numpy as jnp
from jax import lax
from jax.sharding import PartitionSpec as P

STRIDE = 8
RADIUS = 8
POWER = 6
ITERS = 10
highest = lax.Precision.HIGHEST
ridge_term = 0.1
shrink = 0.05
epsilon = 1e-06


def shifted(value, axis, steps):
    count = lax.axis_size(axis)
    first, last = (max(0, -steps), min(count, count - steps))
    return lax.ppermute(value, axis, [(source, source + steps) for source in range(first, last)])


def tap_table(length, centers_count, offset):
    cell_pos = jnp.arange(length, dtype=jnp.float32)
    centers = STRIDE * jnp.arange(centers_count, dtype=jnp.float32) + offset
    scaled = (cell_pos[:, None] - centers[None, :]) / RADIUS
    inside = jnp.abs(scaled) <= 1.0
    bump_base = 1.0 - scaled * scaled
    zeroth = bump_base * bump_base * bump_base
    first_order = 6.0 * scaled * bump_base * bump_base
    second = -6.0 * bump_base * (1.0 - 5.0 * scaled * scaled)
    stacked = jnp.stack([zeroth, first_order, second])
    return jnp.where(inside[None], stacked, jnp.zeros_like(stacked))


def select_taps(tap_stack, orders):
    pick_rows = (orders[:, None] == jnp.arange(3, dtype=jnp.int32)[None, :]).astype(jnp.float32)
    return jnp.einsum("tj,jlc->tlc", pick_rows, tap_stack, precision=highest)


def monomial_block(fields, powers):
    result = None
    for channel in range(4):
        values = fields[channel].astype(jnp.float32)[None]
        power_here = powers[:, channel][:, None, None, None]
        factor = jnp.where(
            power_here == 0,
            jnp.ones_like(values),
            jnp.where(power_here == 1, values, values * values),
        )
        result = factor if channel == 0 else result * factor
    return result.astype(jnp.bfloat16)


def weak_block(theta_block, x_table, y_table, z_table, orders):
    z_taps = select_taps(z_table, orders[:, 2]).astype(jnp.bfloat16)
    reduced = jnp.einsum("txyz,tzc->txyc", theta_block, z_taps, preferred_element_type=jnp.float32)
    reduced = jnp.einsum(
        "txyc,tyb->txbc", reduced, select_taps(y_table, orders[:, 1]), precision=highest
    )
    return jnp.einsum(
        "txbc,txa->tabc", reduced, select_taps(x_table, orders[:, 0]), precision=highest
    )


def local(snap_start, snap_end, exponents):
    term_count = exponents.shape[0]
    cells_x = snap_start.shape[1]
    height = snap_start.shape[2]
    width_z = snap_start.shape[3]
    x_count = cells_x // STRIDE
    plane_rows = height // STRIDE * (width_z // STRIDE)
    y_table = tap_table(height, height // STRIDE, 0)
    z_table = tap_table(width_z, width_z // STRIDE, 0)
    rim_width = RADIUS - 1
    rim_pair = shifted(
        (snap_start[:, cells_x - rim_width :], snap_end[:, cells_x - rim_width :]), "sub", 1
    )
    first_field = jnp.concatenate([rim_pair[0], snap_start], axis=1)
    last_field = jnp.concatenate([rim_pair[1], snap_end], axis=1)
    x_table = tap_table(cells_x + rim_width, x_count, rim_width)

    def term_block(block_rows):
        theta_block = monomial_block(first_field, block_rows[:, :4])
        return weak_block(theta_block, x_table, y_table, z_table, block_rows[:, 4:])

    library = lax.map(term_block, exponents.reshape(term_count // 8, 8, 7))
    library = library.reshape(term_count, -1, plane_rows)
    change = (last_field.astype(jnp.float32) - first_field.astype(jnp.float32)).astype(jnp.bfloat16)
    targets = weak_block(change, x_table, y_table, z_table, jnp.zeros((4, 3), jnp.int32)).reshape(
        4, -1, plane_rows
    )
    library = library.reshape(term_count, -1)
    targets = targets.reshape(4, -1)
    row_count = library.shape[1]
    lib_count = lax.axis_size("lib")
    sub_count = lax.axis_size("sub")
    lib_index = lax.axis_index("lib")
    total_terms = term_count * lib_count
    total_rows = row_count * sub_count
    shard_piece = lax.all_gather(library.astype(jnp.bfloat16), "lib", axis=0, tiled=True).astype(
        jnp.float32
    )
    squares = jnp.zeros((total_terms,), jnp.float32)
    gram_block = lax.dot_general(
        library,
        shard_piece,
        (((1,), (1,)), ((), ())),
        precision=highest,
        preferred_element_type=jnp.float32,
    )
    gram_rows = gram_block
    squares = lax.dynamic_update_slice_in_dim(
        squares, jnp.sum(shard_piece * shard_piece, axis=1), jnp.int32(0), 0
    )
    gram_rows, squares = (gram_rows, squares)
    cross_terms = lax.dot_general(
        library,
        targets,
        (((1,), (1,)), ((), ())),
        precision=highest,
        preferred_element_type=jnp.float32,
    )
    target_squares = jnp.sum(targets * targets, axis=1)
    gram_rows, squares, cross_terms, target_squares = lax.psum(
        (gram_rows, squares, cross_terms, target_squares), "sub"
    )
    row_offset = lib_index * term_count

    def collect_coef(part_coef):
        return lax.all_gather(part_coef, "lib", axis=1, tiled=True)

    column_scale = jnp.sqrt(squares / total_rows + epsilon)
    target_scale = jnp.sqrt(target_squares / total_rows + epsilon)
    own_scale = lax.dynamic_slice_in_dim(column_scale, row_offset, term_count)
    own_ids = row_offset + jnp.arange(term_count, dtype=jnp.int32)
    identity_part = (own_ids[:, None] == jnp.arange(total_terms, dtype=jnp.int32)[None, :]).astype(
        jnp.float32
    )
    normal_rows = (
        gram_rows / (total_rows * own_scale[:, None] * column_scale[None, :])
        + ridge_term * identity_part
    )
    normal_cross = cross_terms / (total_rows * own_scale[:, None] * target_scale[None, :])
    vector = jnp.full((total_terms,), total_terms ** (-0.5), jnp.float32)
    magnitude = jnp.ones((), jnp.float32)
    for sweep_index in range(POWER):
        applied = lax.all_gather(
            jnp.dot(normal_rows, vector, precision=highest), "lib", axis=0, tiled=True
        )
        magnitude = jnp.sqrt(jnp.sum(applied * applied))
        vector = applied / magnitude
    step_size = 1.0 / magnitude

    def descend(sweep_index, coeffs):
        own_coef = lax.dynamic_slice_in_dim(coeffs, row_offset, term_count, 1)
        gradient = (
            lax.dot_general(
                coeffs,
                normal_rows,
                (((1,), (1,)), ((), ())),
                precision=highest,
                preferred_element_type=jnp.float32,
            )
            - normal_cross.T
        )
        moved_coef = own_coef - step_size * gradient
        shrunk = jnp.sign(moved_coef) * jnp.maximum(jnp.abs(moved_coef) - step_size * shrink, 0.0)
        return collect_coef(shrunk)

    coeffs = lax.fori_loop(0, ITERS, descend, jnp.zeros((4, total_terms), jnp.float32))
    lib_coef = lax.dynamic_slice_in_dim(coeffs, lib_index * term_count, term_count, 1)
    lib_scale = lax.dynamic_slice_in_dim(column_scale, lib_index * term_count, term_count)
    fit_terms = jnp.dot(
        lib_coef / lib_scale[None, :],
        library,
        precision=highest,
        preferred_element_type=jnp.float32,
    )
    fitted = lax.psum_scatter(fit_terms, "lib", scatter_dimension=1, tiled=True)
    return (lib_coef, fitted)


def solution(mesh):
    placed = (P(None, "sub", None, None), P(None, "sub", None, None), P("lib", None))
    return jax.shard_map(
        local,
        mesh=mesh,
        in_specs=placed,
        out_specs=(P(None, "lib"), P(None, ("sub", "lib"))),
        check_vma=False,
    )
```

profile of v0, /device:TPU:1, one launch (start us, length us, event | category | flops | bytes accessed | tf_op | source)
XLA Modules:
  0.0 1000.0 jit_solution(18005302535938893821)
XLA Ops:
  22.3 31.5 %collective-permute-done = bf16[4,7,128,256]{3,2,1,0:T(8,128)(2,1)} collective-permute-done((bf16[4,7,128,256]{3,2,1,0:T(8,128)(2,1)}, bf16[4,7,128,256]{3,2,1,0:T(8,128)(2,1)}, u32[]{:S(2)}, u32[]{:S(2)}) %collective-permute-start) | collective-permute-done | bytes 1835040 | tf_op jit(solution)/shard_map/ppermute | solution.py:19
  55.7 37.4 %collective-permute-done.1 = bf16[4,7,128,256]{3,2,1,0:T(8,128)(2,1)} collective-permute-done((bf16[4,7,128,256]{3,2,1,0:T(8,128)(2,1)}, bf16[4,7,128,256]{3,2,1,0:T(8,128)(2,1)}, u32[]{:S(2)}, u32[]{:S(2)}) %collective-permute-start.1) | collective-permute-done | bytes 1835040 | tf_op jit(solution)/shard_map/ppermute | solution.py:19
  100.4 323.9 %while.22 = (s32[]{:T(128)}, f32[16,8,1,16,32]{4,3,2,1,0:T(8,128)S(1)}, s32[16,8,7]{2,1,0:T(8,128)S(1)}, f32[3,15,1]{1,0,2:T(4,128)S(1)}, f32[3,128,16]{1,0,2:T(...) while((s32[]{:T(128)}, f32[16,8,1,16,32]{4,3,2,1,0:T(8,128)S(1)}, ...), condition=%wide.region_1.2_spmd, body=%wide.region_0.1_spmd.sunk | while | flops 402870656 | bytes 60139724 | solution.py:86
  112.2 7.4 convolution_bitcast_fusion.14
  126.0 6.2 fusion.120
  132.4 7.4 convolution_bitcast_fusion.14
  146.2 6.2 fusion.120
  152.6 7.4 convolution_bitcast_fusion.14
  166.4 6.2 fusion.120
  172.8 7.4 convolution_bitcast_fusion.14
  186.6 6.2 fusion.120
  193.1 7.4 convolution_bitcast_fusion.14
  206.8 6.2 fusion.120
  213.3 7.4 convolution_bitcast_fusion.14
  227.1 6.2 fusion.120
  233.5 7.4 convolution_bitcast_fusion.14
  253.7 7.4 convolution_bitcast_fusion.14
  273.9 7.4 convolution_bitcast_fusion.14
  294.2 7.4 convolution_bitcast_fusion.14
  314.4 7.4 convolution_bitcast_fusion.14
  334.6 7.4 convolution_bitcast_fusion.14
  354.8 7.4 convolution_bitcast_fusion.14
  375.0 7.4 convolution_bitcast_fusion.14
  388.8 6.2 fusion.120
  395.3 7.4 convolution_bitcast_fusion.14
  415.5 7.4 convolution_bitcast_fusion.14
  424.7 8.6 all_gather.26
  435.1 85.1 %all-reduce = (f32[512]{0:T(512)S(1)}, f32[128,4]{0,1:T(4,128)S(1)}, f32[4]{0:T(128)S(1)}) all-reduce(f32[512]{0:T(512)S(1)} %multiply_reduce_fusion, f32[128,4]{0,1:T(4,128)S(1)} %fusion.70, f32[4]{0:T(128)S(1)} %multiply_reduce_fusion.1), channel_id=1, replica_groups=mesh['sub'=32,'lib'=4] {'sub'}, use_global_device_ids=true, to_apply=%region_4.5 | all-reduce | flops 1028 | bytes 8224 | tf_op jit(solution)/shard_map/psum | solution.py:124
  520.6 333.6 %all-reduce.3.cloned.1.call-done = f32[128,512]{1,0:T(8,128)} async-done(((f32[128,512]{1,0:T(8,128)}), f32[128,512]{1,0:T(8,128)}) %all-reduce.3.cloned.1.call-update) | async-done | bytes 262160 | tf_op jit(solution)/shard_map/psum | solution.py:124
  855.6 27.1 %all-gather = f32[4,1,128]{2,1,0:T(1,128)S(1)} all-gather(f32[1,1,128]{2,1,0:T(1,128)S(1)} %convolution_bitcast_fusion.10), channel_id=1, replica_groups=mesh['sub'=32,'lib'=4] {'lib'}, dimensions={0}, use_global_device_ids=true | all-gather | bytes 2560 | tf_op jit(solution)/shard_map/all_gather | solution.py:147
  917.8 54.8 %while.23 = (s32[]{:T(128)}, f32[4,512]{1,0:T(4,128)S(1)}, s32[]{:T(128)}, f32[]{:T(128)}, f32[128,512]{1,0:T(8,128)S(1)}, /*index=5*/f32[128,4]{0,1:T(4,128)S(1)}, f32[]{:T(128)}, s32[]{:T(128)}) while((s32[]{:T(128)}, f32[4,512]{1,0:T(4,128)S(1)}, s32[]{:T(128)}, f32[]{:T(128)}, f32[128,512]{1,0:T(8,128)S(1)}, ...), condition=%wide.region_15.16_spmd, body=%wide.region_14.15_spmd.sunk | while | flops 3149826 | bytes 286817 | solution.py:170
  974.0 17.7 %reduce-scatter.4.cloned.1.call-done = f32[128,4]{1,0:T(8,128)} async-done(((f32[512,4]{1,0:T(8,128)}), f32[128,4]{1,0:T(8,128)}) %reduce-scatter.4.cloned.1.call-update) | async-done | bytes 2064
  (303 shorter events, 276.5 us)
Async XLA Ops:
  7.2 8.9 copy-start.3
  7.2 847.0 %all-reduce.3.cloned.1.call-start = ((), (), s32[]{:S(2)}) async-start(), calls=%async_computation.1 | async-start | bytes 524288 | tf_op jit(solution)/shard_map/psum | solution.py:124
  10.3 11.3 %copy-start.6 = (s32[128,7]{0,1:T(8,128)S(1)}, s32[128,7]{0,1:T(8,128)}, u32[]{:S(2)}) copy-start(s32[128,7]{0,1:T(8,128)} %param.9) | copy-start | bytes 10756
  10.3 43.5 %collective-permute-start = (bf16[4,7,128,256]{3,2,1,0:T(8,128)(2,1)}, bf16[4,7,128,256]{3,2,1,0:T(8,128)(2,1)}, u32[]{:S(2)}, u32[]{:S(2)}) collective-permute-start(bf16[4,7,128,256]{3,2,1,0:T(8,128)(2,1)} %slice.48), channel_id=1, source_target_pairs={{0,4},{4,8},{8,12},{12,16},{16,20},{20,24},{24,28},{28,32},{32,36}... | collective-permute-start | bytes 5505032 | tf_op jit(solution)/shard_map/ppermute | solution.py:19
  17.4 75.7 %collective-permute-start.1 = (bf16[4,7,128,256]{3,2,1,0:T(8,128)(2,1)}, bf16[4,7,128,256]{3,2,1,0:T(8,128)(2,1)}, u32[]{:S(2)}, u32[]{:S(2)}) collective-permute-start(bf16[4,7,128,256]{3,2,1,0:T(8,128)(2,1)} %slice.49), channel_id=1, source_target_pairs={{0,4},{4,8},{8,12},{12,16},{16,20},{20,24},{24,28},{28,32},{32,36}... | collective-permute-start | bytes 5505032 | tf_op jit(solution)/shard_map/ppermute | solution.py:19
  21.5 34.0 %copy-start.2 = (bf16[4,8,128,256]{3,2,1,0:T(8,128)(2,1)S(1)}, bf16[4,8,128,256]{3,2,1,0:T(8,128)(2,1)}, u32[]{:S(2)}) copy-start(bf16[4,8,128,256]{3,2,1,0:T(8,128)(2,1)} %param.7) | copy-start | bytes 6291460
  55.4 37.7 %copy-start.4 = (bf16[4,8,128,256]{3,2,1,0:T(8,128)(2,1)S(1)}, bf16[4,8,128,256]{3,2,1,0:T(8,128)(2,1)}, u32[]{:S(2)}) copy-start(bf16[4,8,128,256]{3,2,1,0:T(8,128)(2,1)} %param.8) | copy-start | bytes 6291460
  55.7 40.2 %copy-start = (bf16[4,15,128,256]{3,2,1,0:T(8,128)(2,1)}, bf16[4,15,128,256]{3,2,1,0:T(8,128)(2,1)S(1)}, u32[]{:S(2)}) copy-start(bf16[4,15,128,256]{3,2,1,0:T(8,128)(2,1)S(1)} %constant_dynamic-update-slice_fusion.1) | copy-start | bytes 11796484
  101.4 3.3 copy-start.1
  121.6 3.3 copy-start.1
  141.8 3.3 copy-start.1
  162.0 3.3 copy-start.1
  182.2 3.3 copy-start.1
  202.5 3.3 copy-start.1
  222.7 3.3 copy-start.1
  242.9 3.3 copy-start.1
  263.1 3.3 copy-start.1
  283.3 3.3 copy-start.1
  303.5 3.3 copy-start.1
  323.8 3.3 copy-start.1
  344.0 3.3 copy-start.1
  364.2 3.3 copy-start.1
  384.4 3.3 copy-start.1
  404.6 3.3 copy-start.1
  520.4 471.3 %reduce-scatter.4.cloned.1.call-start = ((), (), s32[]{:S(2)}) async-start(), calls=%async_computation.2 | async-start | bytes 327680
  972.7 20.5 %copy-start.5 = (f32[4,128]{1,0:T(4,128)}, f32[4,128]{1,0:T(4,128)S(1)}, u32[]{:S(2)}) copy-start(f32[4,128]{1,0:T(4,128)S(1)} %constant_dynamic-slice_fusion) | copy-start | bytes 6148
Sparse Core Ops, SparseCore 0:
  520.5 333.6 all-reduce.2
  974.1 17.5 reduce-scatter.3
where the time goes:
time: 1000 us
  waiting for transfers between devices  420 us (42%)
  matrix products  259 us (26%)
  blocking collectives  198 us (20%)
  other arithmetic  79.8 us (8%)
  between operations  18.6 us (2%)
  local copies, waits for them, and re-layouts  12.4 us (1%)
    psum x1, waiting for transfers between devices, local(): lax.psum((gram_rows, squares, cross_terms, target_squares), 'sub')  334 us
    dot_general x17, matrix products, weak_block(): jnp.einsum('txyc,tyb->txbc', reduced, select_taps(y_table, orders[:, 1]),...  122 us
    dot_general x17, matrix products, weak_block(): jnp.einsum('txyz,tzc->txyc', theta_block, z_taps, preferred_element_type=...  102 us
    psum x1, blocking collectives, local(): lax.psum((gram_rows, squares, cross_terms, target_squares), 'sub')  85.1 us
    broadcast_in_dim x32, other arithmetic, monomial_block(): jnp.where(power_here == 1, values, values * values)  69.6 us
    ppermute x2, waiting for transfers between devices, shifted(): lax.ppermute(value, axis, [(source, source + steps) for source in range(f...  68.9 us
    all_gather x6, blocking collectives, local(): lax.all_gather(jnp.dot(normal_rows, vector, precision=highest), 'lib', ax...  52.5 us
    all_gather x10, blocking collectives, collect_coef(): return lax.all_gather(part_coef, 'lib', axis=1, tiled=True)  52.1 us
  transfers between devices with their start and end apart: 4, of which 4 were waited for; matrix products, arithmetic and copies ran while one was open for 0% of the time, Pallas kernels for 0%

commit v1 on v0

--- a/solution.py
+++ b/solution.py
@@ -11,6 +11,11 @@
 ridge_term = 0.1
 shrink = 0.05
 epsilon = 1e-06
+
+
+def exchange_gather(value, axis, dim):
+    sent = jnp.stack([value] * lax.axis_size(axis))
+    return jnp.concatenate(lax.all_to_all(sent, axis, 0, 0), axis=dim)
 
 
 def shifted(value, axis, steps):
@@ -144,9 +149,7 @@
     vector = jnp.full((total_terms,), total_terms ** (-0.5), jnp.float32)
     magnitude = jnp.ones((), jnp.float32)
     for sweep_index in range(POWER):
-        applied = lax.all_gather(
-            jnp.dot(normal_rows, vector, precision=highest), "lib", axis=0, tiled=True
-        )
+        applied = exchange_gather(jnp.dot(normal_rows, vector, precision=highest), "lib", 0)
         magnitude = jnp.sqrt(jnp.sum(applied * applied))
         vector = applied / magnitude
     step_size = 1.0 / magnitude

time: 1000 us -> 920 us (0.920)
  waiting for transfers between devices: 420 us -> 335 us
    psum x1, waiting for transfers between devices: 334 us -> 243 us  [local(): lax.psum((gram_rows, squares, cross_terms, target_squares), 'sub')]
    all_gather x6 -> x0, blocking collectives: 52.5 us -> none  [local(): lax.all_gather(jnp.dot(normal_rows, vector, precision=highest), 'lib', ax...]
    all_to_all x0 -> x4, blocking collectives: none -> 46 us  [exchange_gather(): return jnp.concatenate(lax.all_to_all(sent, axis, 0, 0), axis=dim)]
  transfers between devices with their start and end apart: 4 -> 6, of which waited for: 4 -> 6; matrix products, arithmetic and copies ran while one was open for 0% -> 1% of each run, Pallas kernels for 0% -> 0%
where the time goes in v1:
time: 920 us; the launch traced here: 919 us
  waiting for transfers between devices  335 us (36%)
  matrix products  259 us (28%)
  blocking collectives  194 us (21%)
  other arithmetic  79.3 us (9%)
  between operations  18.4 us (2%)
  starting transfers between devices  17.1 us (2%)
  local copies, waits for them, and re-layouts  13.7 us (1%)
    psum x1, waiting for transfers between devices, local(): lax.psum((gram_rows, squares, cross_terms, target_squares), 'sub')  243 us
    dot_general x17, matrix products, weak_block(): jnp.einsum('txyc,tyb->txbc', reduced, select_taps(y_table, orders[:, 1]),...  122 us
    dot_general x17, matrix products, weak_block(): jnp.einsum('txyz,tzc->txyc', theta_block, z_taps, preferred_element_type=...  102 us
    psum x1, blocking collectives, local(): lax.psum((gram_rows, squares, cross_terms, target_squares), 'sub')  86.6 us
    broadcast_in_dim x32, other arithmetic, monomial_block(): jnp.where(power_here == 1, values, values * values)  69.6 us
    ppermute x2, waiting for transfers between devices, shifted(): lax.ppermute(value, axis, [(source, source + steps) for source in range(f...  68.9 us
    all_gather x10, blocking collectives, collect_coef(): return lax.all_gather(part_coef, 'lib', axis=1, tiled=True)  52.6 us
    all_to_all x4, blocking collectives, exchange_gather(): return jnp.concatenate(lax.all_to_all(sent, axis, 0, 0), axis=dim)  46 us
  transfers between devices with their start and end apart: 6, of which 6 were waited for; matrix products, arithmetic and copies ran while one was open for 1% of the time, Pallas kernels for 0%

profile of v1, /device:TPU:1, one launch (start us, length us, event | category | flops | bytes accessed | tf_op | source)
XLA Modules:
  0.0 918.9 jit_solution(11021275740745104497)
XLA Ops:
  22.3 31.5 %collective-permute-done = bf16[4,7,128,256]{3,2,1,0:T(8,128)(2,1)} collective-permute-done((bf16[4,7,128,256]{3,2,1,0:T(8,128)(2,1)}, bf16[4,7,128,256]{3,2,1,0:T(8,128)(2,1)}, u32[]{:S(2)}, u32[]{:S(2)}) %collective-permute-start) | collective-permute-done | bytes 1835040 | tf_op jit(solution)/shard_map/ppermute | solution.py:24
  55.7 37.4 %collective-permute-done.1 = bf16[4,7,128,256]{3,2,1,0:T(8,128)(2,1)} collective-permute-done((bf16[4,7,128,256]{3,2,1,0:T(8,128)(2,1)}, bf16[4,7,128,256]{3,2,1,0:T(8,128)(2,1)}, u32[]{:S(2)}, u32[]{:S(2)}) %collective-permute-start.1) | collective-permute-done | bytes 1835040 | tf_op jit(solution)/shard_map/ppermute | solution.py:24
  100.4 324.1 %while.22 = (s32[]{:T(128)}, f32[16,8,1,16,32]{4,3,2,1,0:T(8,128)S(1)}, s32[16,8,7]{2,1,0:T(8,128)S(1)}, f32[3,15,1]{1,0,2:T(4,128)S(1)}, f32[3,128,16]{1,0,2:T(...) while((s32[]{:T(128)}, f32[16,8,1,16,32]{4,3,2,1,0:T(8,128)S(1)}, ...), condition=%wide.region_1.2_spmd, body=%wide.region_0.1_spmd.sunk | while | flops 402870656 | bytes 60139724 | solution.py:91
  112.2 7.4 convolution_bitcast_fusion.14
  126.0 6.2 fusion.120
  132.4 7.4 convolution_bitcast_fusion.14
  146.2 6.2 fusion.120
  152.7 7.4 convolution_bitcast_fusion.14
  172.9 7.4 convolution_bitcast_fusion.14
  193.1 7.4 convolution_bitcast_fusion.14
  206.9 6.2 fusion.120
  213.3 7.4 convolution_bitcast_fusion.14
  227.1 6.2 fusion.120
  233.6 7.4 convolution_bitcast_fusion.14
  253.8 7.4 convolution_bitcast_fusion.14
  274.0 7.4 convolution_bitcast_fusion.14
  287.8 6.2 fusion.120
  294.3 7.4 convolution_bitcast_fusion.14
  308.0 6.2 fusion.120
  314.5 7.4 convolution_bitcast_fusion.14
  334.7 7.4 convolution_bitcast_fusion.14
  355.0 7.4 convolution_bitcast_fusion.14
  368.7 6.2 fusion.120
  375.2 7.4 convolution_bitcast_fusion.14
  395.4 7.4 convolution_bitcast_fusion.14
  415.6 7.4 convolution_bitcast_fusion.14
  424.9 8.6 all_gather.8
  435.4 86.6 %all-reduce = (f32[512]{0:T(512)S(1)}, f32[128,4]{0,1:T(4,128)S(1)}, f32[4]{0:T(128)S(1)}) all-reduce(f32[512]{0:T(512)S(1)} %multiply_reduce_fusion, f32[128,4]{0,1:T(4,128)S(1)} %fusion.70, f32[4]{0:T(128)S(1)} %multiply_reduce_fusion.1), channel_id=1, replica_groups=mesh['sub'=32,'lib'=4] {'sub'}, use_global_device_ids=true, to_apply=%region_4.5 | all-reduce | flops 1028 | bytes 8224 | tf_op jit(solution)/shard_map/psum | solution.py:129
  522.1 242.6 %all-reduce.3.cloned.1.call-done = f32[128,512]{1,0:T(8,128)} async-done(((f32[128,512]{1,0:T(8,128)}), f32[128,512]{1,0:T(8,128)}) %all-reduce.3.cloned.1.call-update) | async-done | bytes 262160 | tf_op jit(solution)/shard_map/psum | solution.py:129
  766.0 27.6 %all_to_all.36 = f32[4,1,128]{2,1,0:T(1,128)S(1)} all-to-all(f32[4,1,128]{2,1,0:T(1,128)S(1)} %stack.32), channel_id=1, replica_groups=mesh['sub'=32,'lib'=4] {'lib'}, dimensions={0} | all-to-all | bytes 4096 | tf_op jit(solution)/shard_map/all_to_all | solution.py:18
  836.2 55.3 %while.23 = (s32[]{:T(128)}, f32[4,512]{1,0:T(4,128)S(1)}, s32[]{:T(128)}, f32[]{:T(128)}, f32[128,512]{1,0:T(8,128)S(1)}, /*index=5*/f32[128,4]{0,1:T(4,128)S(1)}, f32[]{:T(128)}, s32[]{:T(128)}) while((s32[]{:T(128)}, f32[4,512]{1,0:T(4,128)S(1)}, s32[]{:T(128)}, f32[]{:T(128)}, f32[128,512]{1,0:T(8,128)S(1)}, ...), condition=%wide.region_15.16_spmd, body=%wide.region_14.15_spmd.sunk | while | flops 3149826 | bytes 286817 | solution.py:173
  892.9 17.7 %reduce-scatter.4.cloned.1.call-done = f32[128,4]{1,0:T(8,128)} async-done(((f32[512,4]{1,0:T(8,128)}), f32[128,4]{1,0:T(8,128)}) %reduce-scatter.4.cloned.1.call-update) | async-done | bytes 2064
  (311 shorter events, 284.6 us)
Async XLA Ops:
  7.2 8.9 copy-start.3
  7.2 757.5 %all-reduce.3.cloned.1.call-start = ((), (), s32[]{:S(2)}) async-start(), calls=%async_computation.7 | async-start | bytes 524288 | tf_op jit(solution)/shard_map/psum | solution.py:129
  10.3 11.3 %copy-start.6 = (s32[128,7]{0,1:T(8,128)S(1)}, s32[128,7]{0,1:T(8,128)}, u32[]{:S(2)}) copy-start(s32[128,7]{0,1:T(8,128)} %param.9) | copy-start | bytes 10756
  10.3 43.5 %collective-permute-start = (bf16[4,7,128,256]{3,2,1,0:T(8,128)(2,1)}, bf16[4,7,128,256]{3,2,1,0:T(8,128)(2,1)}, u32[]{:S(2)}, u32[]{:S(2)}) collective-permute-start(bf16[4,7,128,256]{3,2,1,0:T(8,128)(2,1)} %slice.48), channel_id=1, source_target_pairs={{0,4},{4,8},{8,12},{12,16},{16,20},{20,24},{24,28},{28,32},{32,36}... | collective-permute-start | bytes 5505032 | tf_op jit(solution)/shard_map/ppermute | solution.py:24
  17.4 75.7 %collective-permute-start.1 = (bf16[4,7,128,256]{3,2,1,0:T(8,128)(2,1)}, bf16[4,7,128,256]{3,2,1,0:T(8,128)(2,1)}, u32[]{:S(2)}, u32[]{:S(2)}) collective-permute-start(bf16[4,7,128,256]{3,2,1,0:T(8,128)(2,1)} %slice.49), channel_id=1, source_target_pairs={{0,4},{4,8},{8,12},{12,16},{16,20},{20,24},{24,28},{28,32},{32,36}... | collective-permute-start | bytes 5505032 | tf_op jit(solution)/shard_map/ppermute | solution.py:24
  21.5 34.0 %copy-start.2 = (bf16[4,8,128,256]{3,2,1,0:T(8,128)(2,1)S(1)}, bf16[4,8,128,256]{3,2,1,0:T(8,128)(2,1)}, u32[]{:S(2)}) copy-start(bf16[4,8,128,256]{3,2,1,0:T(8,128)(2,1)} %param.7) | copy-start | bytes 6291460
  55.4 37.7 %copy-start.4 = (bf16[4,8,128,256]{3,2,1,0:T(8,128)(2,1)S(1)}, bf16[4,8,128,256]{3,2,1,0:T(8,128)(2,1)}, u32[]{:S(2)}) copy-start(bf16[4,8,128,256]{3,2,1,0:T(8,128)(2,1)} %param.8) | copy-start | bytes 6291460
  55.7 40.2 %copy-start = (bf16[4,15,128,256]{3,2,1,0:T(8,128)(2,1)}, bf16[4,15,128,256]{3,2,1,0:T(8,128)(2,1)S(1)}, u32[]{:S(2)}) copy-start(bf16[4,15,128,256]{3,2,1,0:T(8,128)(2,1)S(1)} %constant_dynamic-update-slice_fusion.1) | copy-start | bytes 11796484
  101.4 3.3 copy-start.1
  121.6 3.3 copy-start.1
  141.8 3.3 copy-start.1
  162.0 3.3 copy-start.1
  182.3 3.3 copy-start.1
  202.5 3.3 copy-start.1
  222.7 3.3 copy-start.1
  243.0 3.3 copy-start.1
  263.2 3.3 copy-start.1
  283.4 3.3 copy-start.1
  303.7 3.3 copy-start.1
  323.9 3.3 copy-start.1
  344.1 3.3 copy-start.1
  364.3 3.3 copy-start.1
  384.6 3.3 copy-start.1
  404.8 3.3 copy-start.1
  819.0 6.9 all-to-all-start.4
  828.1 6.9 all-to-all-start.5
  832.0 78.6 %reduce-scatter.4.cloned.1.call-start = ((), (), s32[]{:S(2)}) async-start(), calls=%async_computation.8 | async-start | bytes 327680
  891.6 20.5 %copy-start.5 = (f32[4,128]{1,0:T(4,128)}, f32[4,128]{1,0:T(4,128)S(1)}, u32[]{:S(2)}) copy-start(f32[4,128]{1,0:T(4,128)S(1)} %constant_dynamic-slice_fusion) | copy-start | bytes 6148
Sparse Core Ops, SparseCore 0:
  435.5 329.1 all-reduce.2
  893.0 17.5 reduce-scatter.3
